TPU v7x, 32 devices: a whole 2x2x4 slice. The times are simulated.
32 devices in a mesh: batch: 8 (over y, x, core), tile: 4 (over z).
Axes of the slice: x: 2, y: 2, z: 4, core: 2. Of those that a mesh axis runs over, the one named last changes fastest.
Arguments:
- object_field: float32 [2, 2, 3072, 1536], P(None, None, 'batch', 'tile'), may hold values from -6 to 6
- probe_wave: bfloat16 [2, 256, 256], replicated, may hold values from -4.1875 to 4.1875
- intensities: float32 [512, 256, 256], P(('batch', 'tile')), may hold values from 0 to 4
- owner_rows: int32 [512, 1], P(('batch', 'tile')), may hold values from 0 to 7; in each aligned block of 16 rows (0 to 15, 16 to 31, ...) at most 4 rows name the same one
- offsets: int32 [512, 2], P(('batch', 'tile')), may hold values from 0 to 128
Outputs:
- new_object: float32 [2, 2, 3072, 1536], P(None, None, 'batch', 'tile')
- new_probe: float32 [2, 256, 256], replicated
Inputs may be any that keep to these rules, and one draw needn't show every extreme that they name: `owner_rows`: within the 16 positions of one device, each tile row is named at most 4 times.
All inputs are finite; a program needn't handle non-finite values.
Results may differ from a plain program's by a relative error of at most 0.008.
The roundings to bfloat16 on the way count: a program that leaves them out, or rounds other values in their place, can miss the bound.
Values may be sent and summed in bfloat16 or wider, within the bound.
A program may use at most 192 MiB of HBM per device.

v0:
```python
import math
import jax
import jax.numpy as jnp
from jax import lax
from jax.sharding import PartitionSpec as P

update_rate = 0.1
tv_weight = 12.0
tv_smooth = 1.0
probe_rate = 0.04


def extended(x, sides, width):
    for axis, dim in sides:
        size, length = (lax.axis_size(axis), x.shape[dim])
        up = [(i, (i + 1) % size) for i in range(size)]
        down = [(j, i) for i, j in up]
        last = lax.slice_in_dim(x, length - width, length, axis=dim)
        first = lax.slice_in_dim(x, 0, width, axis=dim)
        before = lax.ppermute(last, axis, up)
        after = lax.ppermute(first, axis, down)
        x = jnp.concatenate([before, x, after], axis=dim)
    return x


def tables(extent):
    counter = jnp.arange(extent, dtype=jnp.int32)
    product = counter[:, None] * counter[None, :] % extent
    angles = product.astype(jnp.float32) * (2.0 * math.pi / extent)
    scaling = 1.0 / math.sqrt(extent)
    cos_table = (jnp.cos(angles) * scaling).astype(jnp.bfloat16)
    sin_table = (-jnp.sin(angles) * scaling).astype(jnp.bfloat16)
    frequency = (counter + extent // 2) % extent - extent // 2
    squared = (frequency * frequency).astype(jnp.float32)
    phases = -(0.5 / extent) * (squared[:, None] + squared[None, :])
    return (cos_table, sin_table, jnp.cos(phases), jnp.sin(phases))


def transform(real_part, imag_part, cos_table, sin_table):
    extent = real_part.shape[0]
    left_stack = jnp.concatenate([cos_table, sin_table], 0)
    right_stack = jnp.concatenate([real_part, imag_part], 1)
    blocks = jnp.dot(left_stack, right_stack, preferred_element_type=jnp.float32)
    mid_real = (blocks[:extent, :extent] - blocks[extent:, extent:]).astype(jnp.bfloat16)
    mid_imag = (blocks[:extent, extent:] + blocks[extent:, :extent]).astype(jnp.bfloat16)
    left_two = jnp.concatenate([mid_real, mid_imag], 0)
    right_two = jnp.concatenate([cos_table, sin_table], 1)
    second = jnp.dot(left_two, right_two, preferred_element_type=jnp.float32)
    out_real = second[:extent, :extent] - second[extent:, extent:]
    out_imag = second[:extent, extent:] + second[extent:, :extent]
    return (out_real, out_imag)


def multislice(object_patch, probe_wave, measured, cos_table, sin_table, prop_real, prop_imag):
    slices = object_patch.shape[0]
    back_sin = -sin_table
    psi_real = probe_wave[0]
    psi_imag = probe_wave[1]
    entering = []
    for slab_index in range(slices):
        trans_real = object_patch[slab_index, 0].astype(jnp.float32)
        trans_imag = object_patch[slab_index, 1].astype(jnp.float32)
        entering.append((psi_real, psi_imag))
        wave_real = psi_real.astype(jnp.float32)
        wave_imag = psi_imag.astype(jnp.float32)
        prod_real = (wave_real * trans_real - wave_imag * trans_imag).astype(jnp.bfloat16)
        prod_imag = (wave_real * trans_imag + wave_imag * trans_real).astype(jnp.bfloat16)
        if slab_index + 1 < slices:
            far_real, far_imag = transform(prod_real, prod_imag, cos_table, sin_table)
            kick_real = (prop_real * far_real - prop_imag * far_imag).astype(jnp.bfloat16)
            kick_imag = (prop_real * far_imag + prop_imag * far_real).astype(jnp.bfloat16)
            near_real, near_imag = transform(kick_real, kick_imag, cos_table, back_sin)
            psi_real = near_real.astype(jnp.bfloat16)
            psi_imag = near_imag.astype(jnp.bfloat16)
    exit_real, exit_imag = transform(prod_real, prod_imag, cos_table, sin_table)
    misfit = 0.5 * (exit_real * exit_real + exit_imag * exit_imag - measured)
    chi_real = (misfit * exit_real).astype(jnp.bfloat16)
    chi_imag = (misfit * exit_imag).astype(jnp.bfloat16)
    grad_real, grad_imag = transform(chi_real, chi_imag, cos_table, back_sin)
    object_grads = [None] * slices
    for slab_index in reversed(range(slices)):
        trans_real = object_patch[slab_index, 0].astype(jnp.float32)
        trans_imag = object_patch[slab_index, 1].astype(jnp.float32)
        wave_real = entering[slab_index][0].astype(jnp.float32)
        wave_imag = entering[slab_index][1].astype(jnp.float32)
        object_grads[slab_index] = jnp.stack(
            [
                grad_real * wave_real + grad_imag * wave_imag,
                grad_imag * wave_real - grad_real * wave_imag,
            ]
        )
        dpsi_real = grad_real * trans_real + grad_imag * trans_imag
        dpsi_imag = grad_imag * trans_real - grad_real * trans_imag
        if slab_index > 0:
            back_real, back_imag = transform(
                dpsi_real.astype(jnp.bfloat16), dpsi_imag.astype(jnp.bfloat16), cos_table, back_sin
            )
            turn_real = (prop_real * back_real + prop_imag * back_imag).astype(jnp.bfloat16)
            turn_imag = (prop_real * back_imag - prop_imag * back_real).astype(jnp.bfloat16)
            grad_real, grad_imag = transform(turn_real, turn_imag, cos_table, sin_table)
    patch_grad = jnp.stack(object_grads).astype(jnp.bfloat16)
    probe_grad = jnp.stack([dpsi_real, dpsi_imag])
    return (patch_grad, probe_grad)


def tv_local(padded):
    corner_cells = padded[:, :, :-1, :-1]
    down_diff = padded[:, :, 1:, :-1] - corner_cells
    right_diff = padded[:, :, :-1, 1:] - corner_cells
    weight = 1.0 / jnp.sqrt(
        jnp.sum(down_diff * down_diff + right_diff * right_diff, axis=1, keepdims=True) + tv_smooth
    )
    flow_down = weight * down_diff
    flow_right = weight * right_diff
    return (
        flow_down[:, :, :-1, 1:]
        + flow_right[:, :, 1:, :-1]
        - flow_down[:, :, 1:, 1:]
        - flow_right[:, :, 1:, 1:]
    )


def on_device(object_field, probe_wave, intensities, owner_rows, offsets):
    slices = object_field.shape[0]
    tile_rows = object_field.shape[2]
    extent = probe_wave.shape[-1]
    local_rows = intensities.shape[0]
    nbatch = lax.axis_size("batch")
    capacity = max(2, 2 * local_rows // nbatch)
    slots_all = nbatch * capacity
    patch_shape = (slices, 2, extent, extent)
    targets = owner_rows[:, 0]
    serial = jnp.arange(local_rows, dtype=jnp.int32)
    earlier = (targets[:, None] == targets[None, :]) & (serial[None, :] < serial[:, None])
    ranks = jnp.sum(earlier.astype(jnp.int32), axis=1)
    slot_of = targets * capacity + ranks
    request = (
        jnp.zeros((slots_all, 2), jnp.int32).at[slot_of].set(offsets).reshape(nbatch, capacity, 2)
    )
    wanted = lax.all_to_all(request, "batch", split_axis=0, concat_axis=0, tiled=True).reshape(
        slots_all, 2
    )
    anchor = jnp.zeros((), jnp.int32)
    column = lax.all_gather(object_field.astype(jnp.bfloat16), "batch", axis=2, tiled=True)

    def cut_column(target, corner):
        return lax.dynamic_slice(
            column, (anchor, anchor, target * tile_rows + corner[0], corner[1]), patch_shape
        )

    patches_here = jax.vmap(cut_column)(targets, offsets)
    cos_table, sin_table, prop_real, prop_imag = tables(extent)

    def visit_one(probe_local, inputs):
        object_patch, measured = inputs
        patch_grad, probe_grad = multislice(
            object_patch, probe_wave, measured, cos_table, sin_table, prop_real, prop_imag
        )
        return (probe_local + probe_grad, patch_grad)

    probe_local, patch_grads = lax.scan(
        visit_one, jnp.zeros((2, extent, extent), jnp.float32), (patches_here, intensities)
    )
    outgoing = jnp.zeros((slots_all,) + patch_shape, jnp.bfloat16).at[slot_of].set(patch_grads)
    outgoing = outgoing.reshape((nbatch, capacity) + patch_shape)
    returned = lax.all_to_all(outgoing, "batch", split_axis=0, concat_axis=0, tiled=True).reshape(
        (slots_all,) + patch_shape
    )

    def add_slot(slot_idx, field_grad):
        corner = wanted[slot_idx]
        start = (anchor, anchor, corner[0], corner[1])
        current = lax.dynamic_slice(field_grad, start, patch_shape)
        return lax.dynamic_update_slice(
            field_grad, current + returned[slot_idx].astype(jnp.float32), start
        )

    field_grad = lax.fori_loop(0, slots_all, add_slot, jnp.zeros(object_field.shape, jnp.float32))
    probe_total = lax.psum(probe_local, ("batch", "tile"))
    padded = extended(object_field, (("batch", 2), ("tile", 3)), 1)
    new_object = object_field - update_rate * (field_grad + tv_weight * tv_local(padded))
    new_probe = probe_wave.astype(jnp.float32) - probe_rate * probe_total
    return (new_object, new_probe)


def solution(mesh):
    return jax.shard_map(
        on_device,
        mesh=mesh,
        in_specs=(
            P(None, None, "batch", "tile"),
            P(),
            P(("batch", "tile"), None, None),
            P(("batch", "tile"), None),
            P(("batch", "tile"), None),
        ),
        out_specs=(P(None, None, "batch", "tile"), P()),
        check_vma=False,
    )
```

profile of v0, /device:TPU:6, one launch (start us, length us, event | category | flops | bytes accessed | tf_op | source)
XLA Modules:
  0.0 1374.3 jit_solution(8575923773611135377)
XLA Ops:
  18.4 51.1 %all-gather.2.cloned.1.call-done = bf16[2,2,3072,384]{3,2,1,0:T(8,128)(2,1)} async-done(((bf16[2,2,384,384]{3,2,1,0:T(8,128)(2,1)}), bf16[2,2,3072,384]{3,2,1,0:T(8,128)(2,1)}) %all-gather.2.cloned.1.call-update) | async-done | bytes 9437200 | tf_op jit(solution)/shard_map/all_gather | solution.py:144
  73.9 67.6 %while.33 = (s32[]{:T(128)}, bf16[2,2,3072,384]{3,2,1,0:T(8,128)(2,1)}, s32[16,4]{0,1:T(4,128)S(1)}, bf16[16,2,2,256,256]{4,3,2,1,0:T(8,128)(2,1)}, s32[]{:T(128)}) while((s32[]{:T(128)}, bf16[2,2,3072,384]{3,2,1,0:T(8,128)(2,1)}, s32[16,4]{0,1:T(4,128)S(1)}, bf16[16,2,2,256,256]{4,3,2,1,0:T(8,128)(2,1)}, s32[]{:T(128)}) %tuple.156), condition=%wide.while_cond, body=%wide.while_body.sunk | while | flops 2 | bytes 1050225 | solution.py:147
  145.7 224.0 %while.34 = (s32[]{:T(128)}, f32[2,256,256]{1,2,0:T(8,128)}, bf16[16,2,2,256,256]{4,3,2,1,0:T(8,128)(2,1)}, bf16[2,256,256]{1,2,0:T(8,128)(2,1)S(1)}, bf16[16,2,...) while((s32[]{:T(128)}, f32[2,256,256]{1,2,0:T(8,128)}, ...), condition=%wide.region_3.4_spmd.clone.clone.clone.clone, body=%wide.region_2.3_spmd.clone.clone.clone.clone.sunk | while | flops 1626800128 | bytes 54268612 | solution.py:161
  375.6 21.3 %scatter_fusion = bf16[32,2,2,256,256]{4,3,2,1,0:T(8,128)(2,1)} fusion(bf16[32,2,2,256,256]{4,3,2,1,0:T(8,128)(2,1)} %broadcast_in_dim.13, s32[16]{0:T(128)S(1)} %get-tuple-element.547, bf16[16,2,2,256,256]{4,3,2,1,0:T(8,128)(2,1)} %get-tuple-element.229), kind=kCustom, calls=%fused_computation.1 | custom fusion | bytes 25165888 | tf_op jit(solution)/shard_map/scatter | solution.py:164
  409.1 176.3 %collective-permute-done = f32[2,2,1,384]{3,1,2,0:T(2,128)S(1)} collective-permute-done((f32[2,2,1,384]{3,1,2,0:T(2,128)S(1)}, f32[2,2,1,384]{3,1,2,0:T(2,128)S(1)}, u32[]{:S(2)}, u32[]{:S(2)}) %collective-permute-start) | collective-permute-done | bytes 6176 | tf_op jit(solution)/shard_map/ppermute | solution.py:20
  613.5 123.8 %all-reduce.2.cloned.1.call-done = f32[2,256,256]{2,1,0:T(8,128)} async-done(((f32[2,256,256]{2,1,0:T(8,128)}), f32[2,256,256]{2,1,0:T(8,128)}) %all-reduce.2.cloned.1.call-update) | async-done | bytes 524304 | tf_op jit(solution)/shard_map/psum | solution.py:179
  740.7 617.0 %while.32 = (s32[]{:T(128)}, f32[2,2,384,384]{2,3,1,0:T(8,128)}, s32[32,2]{0,1:T(2,128)S(1)}, bf16[32,2,2,256,256]{4,3,2,1,0:T(8,128)(2,1)}, s32[]{:T(128)}, /*index=5*/s32[]{:T(128)}, s32[]{:T(128)}) while((s32[]{:T(128)}, f32[2,2,384,384]{2,3,1,0:T(8,128)}, s32[32,2]{0,1:T(2,128)S(1)}, bf16[32,2,2,256,256]{4,3,2,1,0:T(8,128)(2,1)}, ...), condition=%wide.region_6.7_spmd, body=%wide.region_5.6_spmd.sunk | while | flops 524296 | bytes 11010245 | solution.py:178
  786.7 11.6 dynamic_update_slice.20
  863.3 11.7 dynamic_update_slice.20
  901.9 11.7 dynamic_update_slice.20
  921.5 11.7 dynamic_update_slice.20
  941.1 11.6 dynamic_update_slice.20
  960.6 11.6 dynamic_update_slice.20
  999.1 11.4 dynamic_update_slice.20
  1037.5 11.2 dynamic_update_slice.20
  1056.6 11.7 dynamic_update_slice.20
  1095.2 11.5 dynamic_update_slice.20
  1152.7 11.6 dynamic_update_slice.20
  1191.3 11.7 dynamic_update_slice.20
  1229.9 11.6 dynamic_update_slice.20
  1249.4 11.6 dynamic_update_slice.20
  1288.0 11.7 dynamic_update_slice.20
  1307.6 11.4 dynamic_update_slice.20
  1326.9 11.7 dynamic_update_slice.20
  (979 shorter events, 669.5 us)
Async XLA Ops:
  7.2 2.9 copy-start.6
  7.2 3.0 copy-start.7
  7.2 8.8 copy-start.4
  7.2 62.3 %all-gather.2.cloned.1.call-start = ((), (), s32[]{:S(2)}) async-start(), calls=%async_computation.2 | async-start | bytes 10616832 | tf_op jit(solution)/shard_map/all_gather | solution.py:144
  11.8 385.2 %all-to-all-start = ((s32[8,4,2]{1,2,0:T(2,128)}), s32[8,4,2]{1,2,0:T(2,128)S(1)}, u32[]{:S(2)}, u32[]{:S(2)}) async-start(s32[8,4,2]{1,2,0:T(2,128)} %copy.81), calls=%async_computation | async-start | bytes 16384 | tf_op jit(solution)/shard_map/all_to_all | solution.py:140
  171.4 1.3 copy-start.1
  213.4 1.3 copy-start.1
  241.4 1.3 copy-start.1
  255.4 1.3 copy-start.1
  269.4 1.3 copy-start.1
  283.4 1.3 copy-start.1
  311.4 1.3 copy-start.1
  325.4 1.3 copy-start.1
  353.4 1.4 copy-start.1
  367.4 1.3 copy-start.1
  397.0 7.3 copy-start
  397.0 342.2 %all-to-all-start.1 = ((bf16[8,4,2,2,256,256]{5,4,3,2,1,0:T(8,128)(2,1)}), bf16[8,4,2,2,256,256]{5,4,3,2,1,0:T(8,128)(2,1)}, u32[]{:S(2)}, u32[]{:S(2)}) async-start(bf16[8,4,2,2,256,256]{5,4,3,2,1,0:T(8,128)(2,1)} %bitcast.219), calls=%async_computation.1 | async-start | bytes 33554432 | tf_op jit(solution)/shard_map/all_to_all | solution.py:166
  404.2 333.0 %all-reduce.2.cloned.1.call-start = ((), (), s32[]{:S(2)}) async-start(), calls=%async_computation.3 | async-start | bytes 1048576 | tf_op jit(solution)/shard_map/psum | solution.py:179
  404.3 181.1 %collective-permute-start = (f32[2,2,1,384]{3,1,2,0:T(2,128)S(1)}, f32[2,2,1,384]{3,1,2,0:T(2,128)S(1)}, u32[]{:S(2)}, u32[]{:S(2)}) collective-permute-start(f32[2,2,1,384]{3,1,2,0:T(2,128)S(1)} %copy.111), channel_id=1, source_target_pairs={{0,4},{4,8},{8,12},{12,16},{16,20},{20,24},{24,28},{28,0},{1,5},{5... | collective-permute-start | bytes 18440 | tf_op jit(solution)/shard_map/ppermute | solution.py:20
  404.4 181.4 %collective-permute-start.1 = (f32[2,2,1,384]{3,1,2,0:T(2,128)S(1)}, f32[2,2,1,384]{3,1,2,0:T(2,128)S(1)}, u32[]{:S(2)}, u32[]{:S(2)}) collective-permute-start(f32[2,2,1,384]{3,1,2,0:T(2,128)S(1)} %copy.112), channel_id=1, source_target_pairs={{4,0},{8,4},{12,8},{16,12},{20,16},{24,20},{28,24},{0,28},{5,1},{9... | collective-permute-start | bytes 18440 | tf_op jit(solution)/shard_map/ppermute | solution.py:21
  593.7 1.7 copy-start.3
  595.4 8.4 collective-permute-start.2
  596.9 6.9 collective-permute-start.3
  608.9 128.3 %copy-start.5 = (bf16[2,256,256]{2,1,0:T(8,128)(2,1)S(1)}, bf16[2,256,256]{2,1,0:T(8,128)(2,1)}, u32[]{:S(2)}) copy-start(bf16[2,256,256]{2,1,0:T(8,128)(2,1)} %param.10) | copy-start | bytes 786436
  (22 other events, 20.5 us)
Sparse Core Ops, SparseCore 0:
  10.5 58.9 all-gather.1
  609.0 128.1 all-reduce.1
where the time goes:
time: 1390 us; the launch traced here: 1370 us
  local copies, waits for them, and re-layouts  663 us (48%)
  waiting for transfers between devices  351 us (25%)
  other arithmetic  143 us (10%)
  loops' own time  121 us (9%)
  matrix products  64.9 us (5%)
  starting transfers between devices  17.1 us (1%)
  between operations  14.2 us (1%)
    dynamic_update_slice x64, local copies, waits for them, and re-layouts, add_slot(): lax.dynamic_update_slice(field_grad, current + returned[slot_idx].astype(...  374 us
    ppermute x2, waiting for transfers between devices, extended(): before = lax.ppermute(last, axis, up)  176 us
    psum x1, waiting for transfers between devices, on_device(): probe_total = lax.psum(probe_local, ('batch', 'tile'))  124 us
    another operation x1, loops' own time, on_device(): lax.fori_loop(0, slots_all, add_slot, jnp.zeros(object_field.shape, jnp.f...  118 us
    dynamic_slice x64, local copies, waits for them, and re-layouts, add_slot(): current = lax.dynamic_slice(field_grad, start, patch_shape)  67.6 us
    gather x48, local copies, waits for them, and re-layouts  67.5 us
    all_gather x1, waiting for transfers between devices, on_device(): lax.all_gather(object_field.astype(jnp.bfloat16), 'batch', axis=2, tiled=...  51.1 us
    dynamic_slice x64, local copies, waits for them, and re-layouts, on_device(): lax.scan(visit_one, jnp.zeros((2, extent, extent), jnp.float32), (patches...  49.4 us
  transfers between devices with their start and end apart: 8, of which 3 were waited for; matrix products, arithmetic and copies ran while one was open for 25% of the time, Pallas kernels for 0%

commit v1 on v0

--- a/solution.py
+++ b/solution.py
@@ -3,11 +3,17 @@
 import jax.numpy as jnp
 from jax import lax
 from jax.sharding import PartitionSpec as P
+from jax.lax import all_gather
 
 update_rate = 0.1
 tv_weight = 12.0
 tv_smooth = 1.0
 probe_rate = 0.04
+
+
+def compute_the_limits(local_values):
+    taken_in = jnp.sum(all_gather(local_values, ("batch", "tile")), axis=0)
+    return taken_in
 
 
 def extended(x, sides, width):
@@ -176,7 +182,7 @@
         )
 
     field_grad = lax.fori_loop(0, slots_all, add_slot, jnp.zeros(object_field.shape, jnp.float32))
-    probe_total = lax.psum(probe_local, ("batch", "tile"))
+    probe_total = compute_the_limits(probe_local)
     padded = extended(object_field, (("batch", 2), ("tile", 3)), 1)
     new_object = object_field - update_rate * (field_grad + tv_weight * tv_local(padded))
     new_probe = probe_wave.astype(jnp.float32) - probe_rate * probe_total

time: 1390 us -> 1320 us (0.950)
  waiting for transfers between devices: 351 us -> 272 us
    psum x1 -> x0, waiting for transfers between devices: 124 us -> none  [on_device(): probe_total = lax.psum(probe_local, ('batch', 'tile'))]
    ppermute x2, waiting for transfers between devices: 176 us -> 221 us  [extended(): before = lax.ppermute(last, axis, up)]
  transfers between devices with their start and end apart: 8 -> 8, of which waited for: 3 -> 2; matrix products, arithmetic and copies ran while one was open for 25% -> 66% of each run, Pallas kernels for 0% -> 0%
where the time goes in v1:
time: 1320 us; the launch traced here: 1300 us
  local copies, waits for them, and re-layouts  669 us (51%)
  waiting for transfers between devices  272 us (21%)
  other arithmetic  148 us (11%)
  loops' own time  118 us (9%)
  matrix products  64.9 us (5%)
  starting transfers between devices  16.6 us (1%)
  between operations  14.3 us (1%)
    dynamic_update_slice x64, local copies, waits for them, and re-layouts, add_slot(): lax.dynamic_update_slice(field_grad, current + returned[slot_idx].astype(...  376 us
    ppermute x2, waiting for transfers between devices, extended(): before = lax.ppermute(last, axis, up)  221 us
    another operation x1, loops' own time, on_device(): lax.fori_loop(0, slots_all, add_slot, jnp.zeros(object_field.shape, jnp.f...  114 us
    gather x48, local copies, waits for them, and re-layouts  67.6 us
    dynamic_slice x64, local copies, waits for them, and re-layouts, add_slot(): current = lax.dynamic_slice(field_grad, start, patch_shape)  67.6 us
    all_gather x1, waiting for transfers between devices, on_device(): lax.all_gather(object_field.astype(jnp.bfloat16), 'batch', axis=2, tiled=...  51.1 us
    dynamic_slice x64, local copies, waits for them, and re-layouts, on_device(): lax.scan(visit_one, jnp.zeros((2, extent, extent), jnp.float32), (patches...  49.4 us
    add x32, other arithmetic, add_slot(): current + returned[slot_idx].astype(jnp.float32)  37.6 us
  transfers between devices with their start and end apart: 8, of which 2 were waited for; matrix products, arithmetic and copies ran while one was open for 66% of the time, Pallas kernels for 0%

profile of v1, /device:TPU:6, one launch (start us, length us, event | category | flops | bytes accessed | tf_op | source)
XLA Modules:
  0.0 1302.4 jit_solution(5085279719609666951)
XLA Ops:
  18.4 51.1 %all-gather.4.cloned.1.call-done = bf16[2,2,3072,384]{3,2,1,0:T(8,128)(2,1)} async-done(((bf16[2,2,384,384]{3,2,1,0:T(8,128)(2,1)}), bf16[2,2,3072,384]{3,2,1,0:T(8,128)(2,1)}) %all-gather.4.cloned.1.call-update) | async-done | bytes 9437200 | tf_op jit(solution)/shard_map/all_gather | solution.py:150
  73.9 67.6 %while.33 = (s32[]{:T(128)}, bf16[2,2,3072,384]{3,2,1,0:T(8,128)(2,1)}, s32[16,4]{0,1:T(4,128)S(1)}, bf16[16,2,2,256,256]{4,3,2,1,0:T(8,128)(2,1)}, s32[]{:T(128)}) while((s32[]{:T(128)}, bf16[2,2,3072,384]{3,2,1,0:T(8,128)(2,1)}, s32[16,4]{0,1:T(4,128)S(1)}, bf16[16,2,2,256,256]{4,3,2,1,0:T(8,128)(2,1)}, s32[]{:T(128)}) %tuple.156), condition=%wide.while_cond, body=%wide.while_body.sunk | while | flops 2 | bytes 1050225 | solution.py:153
  145.8 224.1 %while.34 = (s32[]{:T(128)}, f32[2,256,256]{1,2,0:T(8,128)}, bf16[16,2,2,256,256]{4,3,2,1,0:T(8,128)(2,1)}, bf16[2,256,256]{1,2,0:T(8,128)(2,1)S(1)}, bf16[16,2,...) while((s32[]{:T(128)}, f32[2,256,256]{1,2,0:T(8,128)}, ...), condition=%wide.region_3.4_spmd.clone.clone.clone.clone, body=%wide.region_2.3_spmd.clone.clone.clone.clone.sunk | while | flops 1626800128 | bytes 54268612 | solution.py:167
  375.8 21.3 %scatter_fusion = bf16[32,2,2,256,256]{4,3,2,1,0:T(8,128)(2,1)} fusion(bf16[32,2,2,256,256]{4,3,2,1,0:T(8,128)(2,1)} %broadcast_in_dim.13, s32[16]{0:T(128)S(1)} %get-tuple-element.547, bf16[16,2,2,256,256]{4,3,2,1,0:T(8,128)(2,1)} %get-tuple-element.229), kind=kCustom, calls=%fused_computation.1 | custom fusion | bytes 25165888 | tf_op jit(solution)/shard_map/scatter | solution.py:170
  413.2 220.9 %collective-permute-done = f32[2,2,1,384]{3,1,2,0:T(2,128)S(1)} collective-permute-done((f32[2,2,1,384]{3,1,2,0:T(2,128)S(1)}, f32[2,2,1,384]{3,1,2,0:T(2,128)S(1)}, u32[]{:S(2)}, u32[]{:S(2)}) %collective-permute-start) | collective-permute-done | bytes 6176 | tf_op jit(solution)/shard_map/ppermute | solution.py:26
  659.3 615.8 %while.32 = (s32[]{:T(128)}, f32[2,2,384,384]{2,3,1,0:T(8,128)}, s32[32,2]{0,1:T(2,128)S(1)}, bf16[32,2,2,256,256]{4,3,2,1,0:T(8,128)(2,1)}, s32[]{:T(128)}, /*index=5*/s32[]{:T(128)}, s32[]{:T(128)}) while((s32[]{:T(128)}, f32[2,2,384,384]{2,3,1,0:T(8,128)}, s32[32,2]{0,1:T(2,128)S(1)}, bf16[32,2,2,256,256]{4,3,2,1,0:T(8,128)(2,1)}, ...), condition=%wide.region_6.7_spmd, body=%wide.region_5.6_spmd.sunk | while | flops 524296 | bytes 11010245 | solution.py:184
  705.2 11.7 dynamic_update_slice.20
  781.7 11.7 dynamic_update_slice.20
  820.2 11.7 dynamic_update_slice.20
  839.7 11.7 dynamic_update_slice.20
  859.3 11.6 dynamic_update_slice.20
  878.7 11.6 dynamic_update_slice.20
  917.2 11.4 dynamic_update_slice.20
  955.4 11.3 dynamic_update_slice.20
  974.6 11.7 dynamic_update_slice.20
  1013.1 11.5 dynamic_update_slice.20
  1070.5 11.6 dynamic_update_slice.20
  1109.0 11.7 dynamic_update_slice.20
  1147.5 11.6 dynamic_update_slice.20
  1166.9 11.6 dynamic_update_slice.20
  1186.4 11.3 dynamic_update_slice.20
  1205.5 11.7 dynamic_update_slice.20
  1225.0 11.4 dynamic_update_slice.20
  1244.3 11.7 dynamic_update_slice.20
  (980 shorter events, 668.5 us)
Async XLA Ops:
  7.2 2.9 copy-start.5
  7.2 3.0 copy-start.6
  7.2 8.8 copy-start.4
  7.2 62.3 %all-gather.4.cloned.1.call-start = ((), (), s32[]{:S(2)}) async-start(), calls=%async_computation.2 | async-start | bytes 10616832 | tf_op jit(solution)/shard_map/all_gather | solution.py:150
  11.8 385.3 %all-to-all-start = ((s32[8,4,2]{1,2,0:T(2,128)}), s32[8,4,2]{1,2,0:T(2,128)S(1)}, u32[]{:S(2)}, u32[]{:S(2)}) async-start(s32[8,4,2]{1,2,0:T(2,128)} %copy.85), calls=%async_computation | async-start | bytes 16384 | tf_op jit(solution)/shard_map/all_to_all | solution.py:146
  157.5 1.3 copy-start
  171.5 1.3 copy-start
  213.5 1.3 copy-start
  255.4 1.3 copy-start
  269.5 1.3 copy-start
  283.5 1.3 copy-start
  297.5 1.3 copy-start
  311.5 1.3 copy-start
  325.5 1.3 copy-start
  353.5 1.3 copy-start
  367.5 1.4 copy-start
  397.0 7.2 copy-start.2
  397.0 260.7 %all-to-all-start.1 = ((bf16[8,4,2,2,256,256]{5,4,3,2,1,0:T(8,128)(2,1)}), bf16[8,4,2,2,256,256]{5,4,3,2,1,0:T(8,128)(2,1)}, u32[]{:S(2)}, u32[]{:S(2)}) async-start(bf16[8,4,2,2,256,256]{5,4,3,2,1,0:T(8,128)(2,1)} %bitcast.220), calls=%async_computation.1 | async-start | bytes 33554432 | tf_op jit(solution)/shard_map/all_to_all | solution.py:172
  404.3 883.1 %all-gather.6.cloned.1.call-start = ((), (), s32[]{:S(2)}) async-start(), calls=%async_computation.3 | async-start | bytes 17301504 | tf_op jit(solution)/shard_map/all_gather | solution.py:15
  406.1 228.0 %collective-permute-start = (f32[2,2,1,384]{3,1,2,0:T(2,128)S(1)}, f32[2,2,1,384]{3,1,2,0:T(2,128)S(1)}, u32[]{:S(2)}, u32[]{:S(2)}) collective-permute-start(f32[2,2,1,384]{3,1,2,0:T(2,128)S(1)} %copy.119), channel_id=1, source_target_pairs={{0,4},{4,8},{8,12},{12,16},{16,20},{20,24},{24,28},{28,0},{1,5},{5... | collective-permute-start | bytes 18440 | tf_op jit(solution)/shard_map/ppermute | solution.py:26
  406.3 228.2 %collective-permute-start.1 = (f32[2,2,1,384]{3,1,2,0:T(2,128)S(1)}, f32[2,2,1,384]{3,1,2,0:T(2,128)S(1)}, u32[]{:S(2)}, u32[]{:S(2)}) collective-permute-start(f32[2,2,1,384]{3,1,2,0:T(2,128)S(1)} %copy.120), channel_id=1, source_target_pairs={{4,0},{8,4},{12,8},{16,12},{20,16},{24,20},{28,24},{0,28},{5,1},{9... | collective-permute-start | bytes 18440 | tf_op jit(solution)/shard_map/ppermute | solution.py:27
  641.8 1.7 copy-start.3
  643.4 9.0 collective-permute-start.3
  646.8 5.7 collective-permute-start.2
  (21 other events, 19.2 us)
Sparse Core Ops, SparseCore 0:
  10.5 58.9 all-gather.3
  408.6 231.8 all-gather.5
